TPU v7x, 256 devices: a whole 4x4x8 slice. The times are simulated.
256 devices in a mesh: feat: 16 (over y_lo, x, core), batch: 16 (over y_hi, z).
Axes of the slice: x: 4, y: 4 (y_hi: 2, y_lo: 2; y = y_hi * 2 + y_lo), z: 8, core: 2. Of those that a mesh axis runs over, the one named last changes fastest.
Arguments:
- features: bfloat16 [131072, 4096], P('batch', 'feat'), may hold values from -6 to 6
- src_tile: int32 [256, 2], P('batch'), may hold values from 0 to 7
- rel_type: int32 [256, 2], P('batch'), may hold values from 0 to 3
- timestamps: int32 [32768], P(('batch', 'feat')), may hold values from 0 to 127
- edge_tiles: bfloat16 [4, 128, 1024], replicated, may hold values from -0.1875 to 0.1875
- rel_weight: bfloat16 [4, 4096, 512], P(None, 'feat'), may hold values from -0.09375 to 0.09375
- attn_gain: float32 [512], replicated, may hold values from 0.1 to 1.9
- w_qkv: bfloat16 [512, 1536], replicated, as said below
- w_out: bfloat16 [512, 512], replicated, may hold values from -0.25 to 0.25
- cotangent: bfloat16 [32768, 512], P(('batch', 'feat')), may hold values from -96 to 96
Outputs:
- layer_out: bfloat16 [32768, 512], P(('batch', 'feat'))
- grad_qkv: bfloat16 [512, 1536], replicated
- grad_out: bfloat16 [512, 512], replicated
- grad_gain: bfloat16 [512], replicated
- grad_rel: bfloat16 [4, 4096, 512], P(None, 'feat')
Inputs may be any that keep to these rules, and one draw needn't show every extreme that they name: `src_tile`: index of a source tile within the batch group. `w_qkv`: query, key and value columns in that order along the second dimension.
All inputs are finite; a program needn't handle non-finite values.
Results may differ from a plain program's by a relative error of at most 0.014.
Values may be sent and summed in bfloat16 or wider, within the bound.
No kernel may reach another device: no remote copies, remote signals or barrier semaphores. Data moves between devices by JAX's collectives and lax.ppermute only.
A program may use at most 128 MiB of HBM per device.

v0:
```python
import math
import jax
import jax.numpy as jnp
from jax import lax
from jax.sharding import PartitionSpec as P

D = 512
HEADS = 8
HEAD_DIM = 64
NREL = 4
SLOTS = 2
SBLK = 1024
EPS = 1e-06


def in_blocks(x, dim, devices):
    before, after = (x.shape[:dim], x.shape[dim + 1 :])
    return jnp.moveaxis(x.reshape(*before, devices, -1, *after), dim, 0)


def summed_on_arrival(x, axis, dim):
    pieces = in_blocks(x, dim, lax.axis_size(axis))
    arrived = lax.all_to_all(pieces, axis, split_axis=0, concat_axis=0, tiled=True)
    return arrived.sum(axis=0)


def aggregate(feats, sources_all, kinds_all, edge_tiles):

    def one_block(pair):
        sources, kinds = pair
        parts = []
        for slot in range(SLOTS):
            piece = lax.dynamic_slice_in_dim(feats, sources[slot] * SBLK, SBLK, 0)
            tile = lax.dynamic_index_in_dim(edge_tiles, kinds[slot], 0, keepdims=False)
            parts.append(jnp.dot(tile, piece, preferred_element_type=jnp.float32))
        member = (kinds[:, None] == jnp.arange(NREL, dtype=jnp.int32)[None, :]).astype(jnp.float32)
        merged = member[0][:, None, None] * parts[0][None]
        slot = 1
        merged = merged + member[slot][:, None, None] * parts[slot][None]
        return merged.astype(jnp.bfloat16)

    blocks = lax.map(one_block, (sources_all, kinds_all))
    return jnp.moveaxis(blocks, 1, 0).reshape(NREL, -1, feats.shape[1])


def layer_forward(tokens, gain, w_qkv, w_out, times):
    token_values = tokens.astype(jnp.float32)
    scale = lax.rsqrt(jnp.mean(token_values * token_values, axis=-1, keepdims=True) + EPS)
    normed = (token_values * scale * gain).astype(jnp.bfloat16)
    projected = jnp.dot(normed, w_qkv, preferred_element_type=jnp.float32).astype(jnp.bfloat16)
    length = tokens.shape[0]
    queries = projected[:, :D].reshape(length, HEADS, HEAD_DIM)
    keys = projected[:, D : 2 * D].reshape(length, HEADS, HEAD_DIM)
    contents = projected[:, 2 * D :].reshape(length, HEADS, HEAD_DIM)
    scores = jnp.einsum(
        "qhd,khd->hqk", queries, keys, preferred_element_type=jnp.float32
    ) / math.sqrt(HEAD_DIM)
    allowed = times[None, :] <= times[:, None]
    scores = jnp.where(allowed[None], scores, -1e30)
    weights = jax.nn.softmax(scores, axis=-1).astype(jnp.bfloat16)
    context = jnp.einsum("hqk,khd->qhd", weights, contents, preferred_element_type=jnp.float32)
    context = context.astype(jnp.bfloat16).reshape(length, D)
    return (token_values + jnp.dot(context, w_out, preferred_element_type=jnp.float32)).astype(
        jnp.bfloat16
    )


def silu_slope(total):
    sigma = jax.nn.sigmoid(total)
    return sigma * (1.0 + total * (1.0 - sigma))


def project_one(relations, rel_weight, relation, start, count):
    rows_part = lax.dynamic_slice_in_dim(relations[relation], start, count, 0)
    return jnp.dot(rows_part, rel_weight[relation], preferred_element_type=jnp.float32)


def project_every(relations, rel_weight, start, count):
    summed = project_one(relations, rel_weight, 0, start, count)
    for relation in range(1, NREL):
        summed = summed + project_one(relations, rel_weight, relation, start, count)
    return summed


def shards(
    features,
    src_tile,
    rel_type,
    timestamps,
    edge_tiles,
    rel_weight,
    attn_gain,
    w_qkv,
    w_out,
    cotangent,
):
    relations = aggregate(features, src_tile, rel_type, edge_tiles)
    own_rows = timestamps.shape[0]
    total = summed_on_arrival(
        project_every(relations, rel_weight, jnp.int32(0), own_rows * lax.axis_size("feat")),
        "feat",
        0,
    )
    hidden = jax.nn.silu(total).astype(jnp.bfloat16)
    layer_out, pullback = jax.vjp(
        lambda a, b, c, d: layer_forward(a, b, c, d, timestamps), hidden, attn_gain, w_qkv, w_out
    )
    d_hidden, d_gain, d_qkv, d_out = pullback(cotangent)
    d_total = (d_hidden.astype(jnp.float32) * silu_slope(total)).astype(jnp.bfloat16)
    piece = lax.all_gather(d_total, "feat", axis=0, tiled=True)
    columns = lax.slice_in_dim(relations, 0, piece.shape[0], axis=1)
    rel_terms = lax.dot_general(
        columns, piece, (((1,), (0,)), ((), ())), preferred_element_type=jnp.float32
    )
    grad_rel = lax.psum(rel_terms, "batch").astype(jnp.bfloat16)
    terms = (d_qkv.astype(jnp.float32), d_out.astype(jnp.float32), d_gain)
    sums = lax.psum((terms[0], terms[1], terms[2]), ("feat", "batch"))
    grad_qkv = sums[0].astype(jnp.bfloat16)
    grad_out = sums[1].astype(jnp.bfloat16)
    grad_gain = sums[2].astype(jnp.bfloat16)
    return (layer_out, grad_qkv, grad_out, grad_gain, grad_rel)


def solution(mesh):
    in_specs = (
        P("batch", "feat"),
        P("batch", None),
        P("batch", None),
        P(("batch", "feat")),
        P(),
        P(None, "feat", None),
        P(),
        P(),
        P(),
        P(("batch", "feat"), None),
    )
    out_specs = (P(("batch", "feat"), None), P(), P(), P(), P(None, "feat", None))
    return jax.shard_map(shards, mesh=mesh, in_specs=in_specs, out_specs=out_specs, check_vma=False)
```

profile of v0, /device:TPU:16, one launch (start us, length us, event | category | flops | bytes accessed | tf_op | source)
XLA Modules:
  0.0 512.9 jit_solution(11323617679978035870)
XLA Ops:
  8.1 171.9 %while.10 = (s32[]{:T(128)}, bf16[16,4,128,256]{3,2,0,1:T(8,128)(2,1)}, s32[16,2]{1,0:T(8,128)S(1)}, bf16[4,128,1024]{2,1,0:T(8,128)(2,1)}, s32[16,2]{0,1:T(2,12...) while((s32[]{:T(128)}, ...), condition=%wide.region_1.2_spmd, body=%wide.region_0.1_spmd.sunk | while | flops 134742048 | bytes 2360321 | solution.py:42
  12.5 1.4 fusion.102
  23.3 1.4 fusion.102
  34.0 1.4 fusion.102
  44.8 1.4 fusion.102
  55.5 1.4 fusion.102
  66.3 1.4 fusion.102
  77.0 1.4 fusion.102
  130.7 1.4 fusion.102
  152.2 1.4 fusion.102
  179.9 2.7 fusion.51
  184.8 2.7 add_add_fusion
  187.6 5.3 %all-to-all-start = ((f32[16,128,512]{2,1,0:T(8,128)}), f32[16,128,512]{2,1,0:T(8,128)}, u32[]{:S(2)}, u32[]{:S(2)}) async-start(f32[16,128,512]{2,1,0:T(8,128)} %bitcast.108), calls=%async_computation | async-start | bytes 8388608 | tf_op jit(solution)/shard_map/all_to_all | solution.py:23
  194.1 55.0 %all-to-all-done = f32[16,128,512]{2,1,0:T(8,128)} async-done(((f32[16,128,512]{2,1,0:T(8,128)}), f32[16,128,512]{2,1,0:T(8,128)}, u32[]{:S(2)}, u32[]{:S(2)}) %all-to-all-start) | async-done | bytes 4194336 | tf_op jit(solution)/shard_map/all_to_all | solution.py:23
  249.1 2.6 reduce_sum.51
  253.2 1.9 fusion.53
  256.5 2.1 multiply_reduce_fusion
  258.6 1.6 convolution_convert_fusion.5
  260.3 1.6 convolution_convert_fusion.4
  263.6 2.3 fusion.13
  265.9 1.5 convolution_convert_fusion.8
  268.6 138.7 %all-reduce.7 = (bf16[512,1536]{1,0:T(8,128)(2,1)}, bf16[512,512]{1,0:T(8,128)(2,1)}, bf16[512]{0:T(512)(128)(2,1)}) all-reduce(f32[512,1536]{1,0:T(8,128)} %fusion.13, f32[512,512]{1,0:T(8,128)S(1)} %fusion.17, f32[512]{0:T(512)S(1)} %get-tuple-element.51), channel_id=1, replica_groups=mesh['feat'=16,'batch'=16] {'feat','batch'}, use_global_device_ids=true, to_apply=%region_7.8 | all-reduce | flops 1049088 | bytes 6294528 | tf_op jit(solution)/shard_map/psum | solution.py:117
  407.3 6.6 %fusion.14 = f32[4,256,512]{2,1,0:T(8,128)} fusion(bf16[4,2048,256]{2,1,0:T(8,128)(2,1)} %bitcast.110, bf16[2048,512]{1,0:T(8,128)(2,1)} %all-gather.2.cloned.1.call-done), kind=kOutput, calls=%fused_computation.23 | convolution fusion | flops 2147483648 | bytes 8388608 | tf_op jit(solution)/shard_map/dot_general | solution.py:112
  413.9 92.2 %all-reduce.6 = bf16[4,256,512]{2,1,0:T(8,128)(2,1)} all-reduce(f32[4,256,512]{2,1,0:T(8,128)} %fusion.14), channel_id=1, replica_groups=mesh['feat'=16,'batch'=16] {'batch'}, use_global_device_ids=true, to_apply=%region_12.13 | all-reduce | flops 524288 | bytes 3145728 | tf_op jit(solution)/shard_map/psum | solution.py:115
  (197 shorter events, 85.8 us)
Async XLA Ops:
  7.2 245.3 %copy-start = (bf16[512,1536]{1,0:T(8,128)(2,1)S(1)}, bf16[512,1536]{1,0:T(8,128)(2,1)}, u32[]{:S(2)}) copy-start(bf16[512,1536]{1,0:T(8,128)(2,1)} %param.19) | copy-start | bytes 4718596
  179.9 2.8 copy-start.3
  187.6 5.4 %copy-start.1 = (bf16[512,512]{1,0:T(8,128)(2,1)S(1)}, bf16[512,512]{1,0:T(8,128)(2,1)}, u32[]{:S(2)}) copy-start(bf16[512,512]{1,0:T(8,128)(2,1)} %param.20) | copy-start | bytes 1572868
  187.6 5.4 %copy-start.2 = (bf16[128,512]{1,0:T(8,128)(2,1)S(1)}, bf16[128,512]{1,0:T(8,128)(2,1)}, u32[]{:S(2)}) copy-start(bf16[128,512]{1,0:T(8,128)(2,1)} %param.21) | copy-start | bytes 393220
  187.6 5.8 %copy-start.7 = (s32[128]{0:T(128)S(1)}, s32[128]{0:T(128)}, u32[]{:S(2)}) copy-start(s32[128]{0:T(128)} %param.15) | copy-start | bytes 1540
  187.6 61.6 %all-to-all-start = ((f32[16,128,512]{2,1,0:T(8,128)}), f32[16,128,512]{2,1,0:T(8,128)}, u32[]{:S(2)}, u32[]{:S(2)}) async-start(f32[16,128,512]{2,1,0:T(8,128)} %bitcast.108), calls=%async_computation | async-start | bytes 8388608 | tf_op jit(solution)/shard_map/all_to_all | solution.py:23
  192.9 59.6 %copy-start.6 = (f32[512]{0:T(512)S(1)}, f32[512]{0:T(512)}, u32[]{:S(2)}) copy-start(f32[512]{0:T(512)} %param.18) | copy-start | bytes 6148
  192.9 214.4 %all-gather.2.cloned.1.call-start = ((), (), s32[]{:S(2)}) async-start(), calls=%async_computation.1 | async-start | bytes 2228224 | tf_op jit(solution)/shard_map/all_gather | solution.py:110
  251.9 0.5 copy-start.8
  253.0 7.2 %copy-start.4 = (bf16[128,512]{0,1:T(8,128)(2,1)}, bf16[128,512]{0,1:T(8,128)(2,1)S(1)}, u32[]{:S(2)}) copy-start(bf16[128,512]{0,1:T(8,128)(2,1)S(1)} %copy.30) | copy-start | bytes 393220
  253.2 7.1 %copy-start.5 = (bf16[128,512]{0,1:T(8,128)(2,1)}, bf16[128,512]{0,1:T(8,128)(2,1)S(1)}, u32[]{:S(2)}) copy-start(bf16[128,512]{0,1:T(8,128)(2,1)S(1)} %copy.31) | copy-start | bytes 393220
  258.6 4.0 copy-start.9
Sparse Core Ops, SparseCore 0:
  263.7 39.7 all-gather.1
where the time goes:
time: 516 us; the launch traced here: 513 us
  blocking collectives  231 us (45%)
  loops' own time  83.6 us (16%)
  matrix products  70 us (14%)
  waiting for transfers between devices  55.1 us (11%)
  local copies, waits for them, and re-layouts  34.8 us (7%)
  other arithmetic  18.9 us (4%)
  between operations  14.3 us (3%)
  starting transfers between devices  5.35 us (1%)
    psum x1, blocking collectives, shards(): sums = lax.psum((terms[0], terms[1], terms[2]), ('feat', 'batch'))  139 us
    psum x1, blocking collectives, shards(): grad_rel = lax.psum(rel_terms, 'batch').astype(jnp.bfloat16)  92.2 us
    another operation x1, loops' own time, aggregate(): blocks = lax.map(one_block, (sources_all, kinds_all))  83.6 us
    all_to_all x1, waiting for transfers between devices, summed_on_arrival(): lax.all_to_all(pieces, axis, split_axis=0, concat_axis=0, tiled=True)  55 us
    dot_general x32, matrix products, one_block(): parts.append(jnp.dot(tile, piece, preferred_element_type=jnp.float32))  43.6 us
    dynamic_update_slice x16, other arithmetic, aggregate(): blocks = lax.map(one_block, (sources_all, kinds_all))  13.4 us
    dynamic_slice x32, local copies, waits for them, and re-layouts, aggregate(): blocks = lax.map(one_block, (sources_all, kinds_all))  12.2 us
  transfers between devices with their start and end apart: 2, of which 1 were waited for; matrix products, arithmetic and copies ran while one was open for 1% of the time, Pallas kernels for 0%

commit v1 on v0

--- a/solution.py
+++ b/solution.py
@@ -112,7 +112,7 @@
     rel_terms = lax.dot_general(
         columns, piece, (((1,), (0,)), ((), ())), preferred_element_type=jnp.float32
     )
-    grad_rel = lax.psum(rel_terms, "batch").astype(jnp.bfloat16)
+    grad_rel = jnp.sum(lax.all_gather(rel_terms, "batch"), axis=0).astype(jnp.bfloat16)
     terms = (d_qkv.astype(jnp.float32), d_out.astype(jnp.float32), d_gain)
     sums = lax.psum((terms[0], terms[1], terms[2]), ("feat", "batch"))
     grad_qkv = sums[0].astype(jnp.bfloat16)

time: 516 us -> 763 us (1.48)
  waiting for transfers between devices: 55.1 us -> 182 us
  blocking collectives: 231 us -> 331 us
  other arithmetic: 18.9 us -> 32.8 us
    psum x1, blocking collectives: 139 us -> 331 us  [shards(): sums = lax.psum((terms[0], terms[1], terms[2]), ('feat', 'batch'))]
    psum x1 -> x0, blocking collectives: 92.2 us -> none  [shards(): grad_rel = lax.psum(rel_terms, 'batch').astype(jnp.bfloat16)]
    all_gather x0 -> x1, waiting for transfers between devices: none -> 89 us  [shards(): lax.all_gather(rel_terms, 'batch')]
    all_gather x1, waiting for transfers between devices: 0.01 us -> 38.3 us  [shards(): piece = lax.all_gather(d_total, 'feat', axis=0, tiled=True)]
    reduce_sum x0 -> x1, other arithmetic: none -> 13.8 us  [shards(): jnp.sum(lax.all_gather(rel_terms, 'batch'), axis=0).astype(jnp.bfloat16)]
  transfers between devices with their start and end apart: 2 -> 3, of which waited for: 1 -> 3; matrix products, arithmetic and copies ran while one was open for 1% -> 1% of each run, Pallas kernels for 0% -> 0%
where the time goes in v1:
time: 763 us; the launch traced here: 755 us
  blocking collectives  331 us (43%)
  waiting for transfers between devices  182 us (24%)
  loops' own time  83.4 us (11%)
  matrix products  70.8 us (9%)
  local copies, waits for them, and re-layouts  34.7 us (5%)
  other arithmetic  32.8 us (4%)
  between operations  14.3 us (2%)
    psum x1, blocking collectives, shards(): sums = lax.psum((terms[0], terms[1], terms[2]), ('feat', 'batch'))  331 us
    all_gather x1, waiting for transfers between devices, shards(): lax.all_gather(rel_terms, 'batch')  89 us
    another operation x1, loops' own time, aggregate(): blocks = lax.map(one_block, (sources_all, kinds_all))  83.4 us
    all_to_all x1, waiting for transfers between devices, summed_on_arrival(): lax.all_to_all(pieces, axis, split_axis=0, concat_axis=0, tiled=True)  55.1 us
    dot_general x32, matrix products, one_block(): parts.append(jnp.dot(tile, piece, preferred_element_type=jnp.float32))  43.6 us
    all_gather x1, waiting for transfers between devices, shards(): piece = lax.all_gather(d_total, 'feat', axis=0, tiled=True)  38.3 us
  transfers between devices with their start and end apart: 3, of which 3 were waited for; matrix products, arithmetic and copies ran while one was open for 1% of the time, Pallas kernels for 0%

profile of v1, /device:TPU:16, one launch (start us, length us, event | category | flops | bytes accessed | tf_op | source)
XLA Modules:
  0.0 754.6 jit_solution(4720020433054538425)
XLA Ops:
  8.1 171.6 %while.10 = (s32[]{:T(128)}, bf16[16,4,128,256]{3,2,0,1:T(8,128)(2,1)}, s32[16,2]{1,0:T(8,128)S(1)}, bf16[4,128,1024]{2,1,0:T(8,128)(2,1)}, s32[16,2]{0,1:T(2,12...) while((s32[]{:T(128)}, ...), condition=%wide.region_1.2_spmd, body=%wide.region_0.1_spmd.sunk | while | flops 134742048 | bytes 2359821 | solution.py:42
  16.6 1.4 fusion.102
  27.3 1.4 fusion.102
  38.0 1.4 fusion.102
  48.7 1.4 fusion.102
  59.5 1.4 fusion.102
  113.1 1.4 fusion.102
  123.8 1.4 fusion.102
  177.4 1.4 fusion.102
  179.7 2.7 fusion.51
  184.5 2.7 add_add_fusion
  187.3 5.3 all-to-all-start
  193.8 55.1 %all-to-all-done = f32[16,128,512]{2,1,0:T(8,128)} async-done(((f32[16,128,512]{2,1,0:T(8,128)}), f32[16,128,512]{2,1,0:T(8,128)}, u32[]{:S(2)}, u32[]{:S(2)}) %all-to-all-start) | async-done | bytes 4194336 | tf_op jit(solution)/shard_map/all_to_all | solution.py:23
  248.9 2.6 reduce_sum.62
  253.0 1.9 fusion.53
  256.2 2.2 multiply_reduce_fusion
  258.4 1.6 convolution_convert_fusion.4
  260.0 1.7 convolution_convert_fusion.5
  263.4 38.3 %all-gather.4.cloned.1.call-done = bf16[2048,512]{1,0:T(8,128)(2,1)} async-done(((bf16[128,512]{1,0:T(8,128)(2,1)}), bf16[2048,512]{1,0:T(8,128)(2,1)}) %all-gather.4.cloned.1.call-update) | async-done | bytes 2097168 | tf_op jit(solution)/shard_map/all_gather | solution.py:110
  301.8 6.6 fusion.14
  310.0 3.3 fusion.13
  314.2 330.8 %all-reduce.5 = (bf16[512,1536]{1,0:T(8,128)(2,1)}, bf16[512,512]{1,0:T(8,128)(2,1)}, bf16[512]{0:T(512)(128)(2,1)}) all-reduce(f32[512,1536]{1,0:T(8,128)} %fusion.13, f32[512,512]{1,0:T(8,128)S(1)} %fusion.17, f32[512]{0:T(512)S(1)} %get-tuple-element.57), channel_id=1, replica_groups=mesh['feat'=16,'batch'=16] {'feat','batch'}, use_global_device_ids=true, to_apply=%region_7.8 | all-reduce | flops 1049088 | bytes 6294528 | tf_op jit(solution)/shard_map/psum | solution.py:117
  645.0 89.0 %all-gather.6.cloned.1.call-done = f32[64,256,512]{2,1,0:T(8,128)} async-done(((f32[4,256,512]{2,1,0:T(8,128)}), f32[64,256,512]{2,1,0:T(8,128)}) %all-gather.6.cloned.1.call-update) | async-done | bytes 33554448 | tf_op jit(solution)/shard_map/all_gather | solution.py:115
  733.9 13.8 %reduce_sum.81 = bf16[4,256,512]{2,1,0:T(8,128)(2,1)} reduce(f32[16,4,256,512]{3,2,1,0:T(8,128)} %bitcast.109, f32[]{:T(128)} %constant.33.clone.1), dimensions={0}, to_apply=%region_12.13 | reduce | flops 7864320 | bytes 34603012 | tf_op jit(solution)/shard_map/reduce_sum | solution.py:115
  (210 shorter events, 88.3 us)
Async XLA Ops:
  7.2 245.0 %copy-start = (bf16[512,1536]{1,0:T(8,128)(2,1)S(1)}, bf16[512,1536]{1,0:T(8,128)(2,1)}, u32[]{:S(2)}) copy-start(bf16[512,1536]{1,0:T(8,128)(2,1)} %param.19) | copy-start | bytes 4718596
  179.7 2.8 copy-start.3
  187.3 5.4 copy-start.1
  187.3 5.4 copy-start.2
  187.3 5.8 copy-start.12
  187.3 61.6 %all-to-all-start = ((f32[16,128,512]{2,1,0:T(8,128)}), f32[16,128,512]{2,1,0:T(8,128)}, u32[]{:S(2)}, u32[]{:S(2)}) async-start(f32[16,128,512]{2,1,0:T(8,128)} %bitcast.110), calls=%async_computation | async-start | bytes 8388608 | tf_op jit(solution)/shard_map/all_to_all | solution.py:23
  192.6 59.6 %copy-start.11 = (f32[512]{0:T(512)S(1)}, f32[512]{0:T(512)}, u32[]{:S(2)}) copy-start(f32[512]{0:T(512)} %param.18) | copy-start | bytes 6148
  192.6 109.2 %all-gather.4.cloned.1.call-start = ((), (), s32[]{:S(2)}) async-start(), calls=%async_computation.1 | async-start | bytes 2228224 | tf_op jit(solution)/shard_map/all_gather | solution.py:110
  251.7 0.5 copy-start.13
  252.8 7.2 copy-start.7
  252.9 7.1 copy-start.9
  256.2 6.3 copy-start.4
  258.4 4.1 copy-start.14
  260.0 48.4 %copy-start.5 = (bf16[8,128,64]{1,2,0:T(8,128)(2,1)}, bf16[8,128,64]{1,2,0:T(8,128)(2,1)S(1)}, u32[]{:S(2)}) copy-start(bf16[8,128,64]{1,2,0:T(8,128)(2,1)S(1)} %convolution_convert_fusion.4) | copy-start | bytes 393220
  261.7 46.7 %copy-start.6 = (bf16[8,128,64]{1,2,0:T(8,128)(2,1)}, bf16[8,128,64]{1,2,0:T(8,128)(2,1)S(1)}, u32[]{:S(2)}) copy-start(bf16[8,128,64]{1,2,0:T(8,128)(2,1)S(1)} %convolution_convert_fusion.5) | copy-start | bytes 393220
  263.4 470.5 %all-gather.6.cloned.1.call-start = ((), (), s32[]{:S(2)}) async-start(), calls=%async_computation.2 | async-start | bytes 35651584 | tf_op jit(solution)/shard_map/all_gather | solution.py:115
  301.8 6.7 copy-start.8
  301.8 6.7 copy-start.10
Sparse Core Ops, SparseCore 0:
  263.5 38.2 all-gather.3
  308.6 425.3 all-gather.5
